TPU v7x, 32 devices: a whole 2x2x4 slice. The times are simulated.
32 devices in a mesh: radial: 1, mode: 32 (over z, y, x, core).
Axes of the slice: x: 2, y: 2, z: 4, core: 2. Of those that a mesh axis runs over, the one named last changes fastest.
Arguments:
- spectral_state: float32 [64, 3, 2, 2, 129], P('mode', None, 'radial'), may hold values from -6 to 6
- synthesis_table: bfloat16 [64, 129, 128], P('mode', None, 'radial'), may hold values from -0.03125 to 0.03125
- low_orders: int32 [64], replicated, may hold values from 0 to 63, each once
- diffusion: float32 [3], replicated, may hold values from 200 to 2000
- coupling: float32 [3], replicated, may hold values from 1 to 4
Outputs:
- updated: float32 [64, 3, 2, 2, 129], P('mode', None, 'radial')
Inputs may be any that keep to these rules, and one draw needn't show every extreme that they name: A permutation: pair j holds the orders low_orders[j] and 127 - low_orders[j].
All inputs are finite; a program needn't handle non-finite values.
Results may differ from a plain program's by a relative error of at most 0.0023.
The roundings to bfloat16 on the way count: a program that leaves them out, or rounds other values in their place, can miss the bound.
Values may be sent and summed in bfloat16 or wider, within the bound.
No kernel may reach another device: no remote copies, remote signals or barrier semaphores. Data moves between devices by JAX's collectives and lax.ppermute only.
A program may use at most 64 MiB of HBM per device.

v0:
```python
import math
import jax
import jax.numpy as jnp
from jax import lax
from jax.sharding import PartitionSpec as P

inner_radius = 0.538
shell_step = 1.0 / 2048.0
block_limit = 384


def with_halo(shard, sides, width):
    for axis, dim in sides:
        count, length = (lax.axis_size(axis), shard.shape[dim])
        up = [(i, (i + 1) % count) for i in range(count - 1)]
        down = [(j, i) for i, j in up]
        last = lax.slice_in_dim(shard, length - width, length, axis=dim)
        first = lax.slice_in_dim(shard, 0, width, axis=dim)
        before = lax.ppermute(last, axis, up)
        after = lax.ppermute(first, axis, down)
        shard = jnp.concatenate([before, shard, after], axis=dim)
    return shard


def pair_layout(lower_orders, rows_total):
    orders_total = rows_total - 1
    row_index = lax.iota(jnp.int32, rows_total)[None, :]
    lower_col = lower_orders[:, None]
    in_lower = row_index < orders_total - lower_col
    degree = jnp.where(in_lower, lower_col + row_index, row_index - 1)
    order_of = jnp.where(in_lower, lower_col, orders_total - 1 - lower_col)
    return (in_lower, degree, order_of)


def body(spectral_state, synthesis_table, low_orders, diffusion, coupling):
    synthesis_table = lax.all_gather(synthesis_table, "radial", axis=2, tiled=True)
    pairs_dev, field_count, shell_count, part_count, rows_total = spectral_state.shape
    half_lat = synthesis_table.shape[2]
    lat_total = 2 * half_lat
    orders_total = rows_total - 1
    lon_total = 3 * orders_total
    mode_count = lax.axis_size("mode")
    column_count = 4 * pairs_dev * mode_count
    own_lower = lax.dynamic_slice_in_dim(low_orders, lax.axis_index("mode") * pairs_dev, pairs_dev)
    in_lower, degree, order_of = pair_layout(own_lower, rows_total)
    parity_even = (degree + order_of) % 2 == 0
    order_mask = jnp.stack([in_lower, jnp.logical_not(in_lower)], axis=1)
    parity_mask = jnp.stack([parity_even, jnp.logical_not(parity_even)], axis=1)
    row_sign = jnp.where(parity_even, 1.0, -1.0).astype(jnp.float32)
    order_float = order_mask.astype(jnp.float32)
    coeffs = spectral_state.astype(jnp.bfloat16)
    all_lower = low_orders.reshape(mode_count, 1, pairs_dev, 1)
    partner = jnp.arange(2, dtype=jnp.int32).reshape(1, 1, 1, 2)
    column_order = jnp.where(partner == 0, all_lower, orders_total - 1 - all_lower)
    column_order = jnp.broadcast_to(column_order, (mode_count, 2, pairs_dev, 2)).reshape(
        column_count
    )
    cosine_rows = jnp.broadcast_to(
        jnp.arange(2, dtype=jnp.int32).reshape(1, 2, 1, 1) == 0, (mode_count, 2, pairs_dev, 2)
    ).reshape(column_count)
    synth_weight = jnp.where(column_order == 0, 1.0, 2.0).astype(jnp.float32)
    block_size = min(block_limit, lon_total)
    block_total = lon_total // block_size
    analysis_scale = 2.0 * math.sqrt(orders_total * rows_total / (lat_total * lon_total))
    spread = (
        coeffs[:, None, :, :, :, None, :]
        * parity_mask.astype(jnp.bfloat16)[:, :, None, None, None, None, :]
        * order_mask.astype(jnp.bfloat16)[:, None, None, None, None, :, :]
    )
    halves = jnp.einsum(
        "pqfsckr,prn->qnsfcpk", spread, synthesis_table, preferred_element_type=jnp.float32
    )
    northern = halves[0] + halves[1]
    southern = (halves[0] - halves[1])[::-1]
    joined = jnp.concatenate([northern, southern], axis=0).astype(jnp.bfloat16)
    pieces = lax.all_to_all(
        joined.reshape(lat_total, shell_count, coeffs.shape[1], 4 * pairs_dev),
        "mode",
        split_axis=0,
        concat_axis=3,
        tiled=True,
    )
    lat_dev = pieces.shape[0]
    item_count = pieces.shape[1]
    row_total = lat_dev * item_count * field_count
    weighted = pieces.reshape(row_total, column_count).astype(jnp.float32) * synth_weight[None, :]
    totals = jnp.zeros((row_total, column_count), jnp.float32)
    for block_at in range(block_total):
        longitude = block_at * block_size + lax.iota(jnp.int32, block_size)
        phase_index = column_order[:, None] * longitude[None, :] % lon_total
        angles = phase_index.astype(jnp.float32) * (2.0 * math.pi / lon_total)
        wave_table = jnp.where(cosine_rows[:, None], jnp.cos(angles), -jnp.sin(angles))
        values = jnp.dot(weighted, wave_table, precision=lax.Precision.HIGHEST)
        values = values.reshape(lat_dev, item_count, field_count, block_size)
        products = jnp.stack(
            [
                values[:, :, 0] * values[:, :, 1],
                values[:, :, 0] * values[:, :, 2],
                values[:, :, 1] * values[:, :, 2],
            ],
            axis=2,
        )
        totals = totals + lax.dot_general(
            products.reshape(row_total, block_size),
            wave_table,
            (((1,), (1,)), ((), ())),
            precision=lax.Precision.HIGHEST,
        )
    answers = (totals * analysis_scale).astype(jnp.bfloat16)
    returned = lax.all_to_all(
        answers.reshape(lat_dev, item_count, field_count, column_count),
        "mode",
        split_axis=3,
        concat_axis=0,
        tiled=True,
    )
    subset_fields = returned.shape[2]
    arranged = returned.reshape(lat_total, shell_count, subset_fields, part_count, pairs_dev, 2)
    from_north = jnp.einsum(
        "prn,nsfcpk->pkfscr",
        synthesis_table,
        arranged[:half_lat],
        preferred_element_type=jnp.float32,
    )
    from_south = jnp.einsum(
        "prn,nsfcpk->pkfscr",
        synthesis_table,
        arranged[half_lat:][::-1],
        preferred_element_type=jnp.float32,
    )
    combined = from_north + row_sign[:, None, None, None, None, :] * from_south
    nonlinear = jnp.sum(combined * order_float[:, :, None, None, None, :], axis=1)
    radial_at = lax.axis_index("radial")
    rate_col = diffusion.reshape(1, field_count, 1, 1)
    strength = coupling.reshape(1, field_count, 1, 1)
    degree_term = degree.astype(jnp.float32)
    degree_term = (degree_term * (degree_term + 1.0))[:, None, None, :] * (shell_step * shell_step)
    with_edges = with_halo(spectral_state.astype(jnp.bfloat16), (("radial", 2),), 1).astype(
        spectral_state.dtype
    )
    diagonals = []
    drives = []
    for shell_at in range(shell_count):
        radius = (
            inner_radius
            + ((radial_at * shell_count + shell_at).astype(jnp.float32) + 0.5) * shell_step
        )
        damping = degree_term / (radius * radius)
        middle = with_edges[:, :, shell_at + 1]
        laplace = (
            with_edges[:, :, shell_at + 2]
            - 2.0 * middle
            + with_edges[:, :, shell_at]
            - damping * middle
        )
        drives.append(middle + rate_col * (laplace + strength * nonlinear[:, :, shell_at]))
        diagonals.append(1.0 + rate_col * (2.0 + damping))
    narrow_zero = jnp.zeros(diagonals[0].shape, jnp.float32)
    wide_zero = jnp.zeros(drives[0].shape, jnp.float32)
    pivot_prev = narrow_zero
    carry_u, carry_v, carry_w = (wide_zero, narrow_zero, narrow_zero)
    pivots, sweep_u, sweep_v, sweep_w = ([], [], [], [])
    for shell_at in range(shell_count):
        denom_at = diagonals[shell_at] + rate_col * pivot_prev
        pivot_prev = -rate_col / denom_at
        first_drive = rate_col if shell_at == 0 else 0.0
        last_drive = rate_col if shell_at == shell_count - 1 else 0.0
        carry_u = (drives[shell_at] + rate_col * carry_u) / denom_at
        carry_v = (first_drive + rate_col * carry_v) / denom_at
        carry_w = (last_drive + rate_col * carry_w) / denom_at
        pivots.append(pivot_prev)
        sweep_u.append(carry_u)
        sweep_v.append(carry_v)
        sweep_w.append(carry_w)
    solved_u, solved_v, solved_w = ([sweep_u[-1]], [sweep_v[-1]], [sweep_w[-1]])
    shell_at = 0
    solved_u.insert(0, sweep_u[shell_at] - pivots[shell_at] * solved_u[0])
    solved_v.insert(0, sweep_v[shell_at] - pivots[shell_at] * solved_v[0])
    solved_w.insert(0, sweep_w[shell_at] - pivots[shell_at] * solved_w[0])
    first_u, last_u = (solved_u[0], solved_u[-1])
    first_v, last_v = (solved_v[0], solved_v[-1])
    first_w, last_w = (solved_w[0], solved_w[-1])
    wide_rows = jnp.stack([first_u, last_u])[None]
    narrow_rows = jnp.stack([first_v, first_w, last_v, last_w])[None]
    wide_all, narrow_all = (
        lax.all_gather(wide_rows, "radial", axis=0, tiled=True),
        lax.all_gather(narrow_rows, "radial", axis=0, tiled=True),
    )
    chain_count = lax.axis_size("radial")
    alpha_now, beta_now = (wide_zero, narrow_zero)
    alphas, betas = ([], [])
    for member in range(chain_count):
        alphas.append(alpha_now)
        betas.append(beta_now)
        peer_first_u, peer_last_u = (wide_all[member, 0], wide_all[member, 1])
        peer_first_v, peer_first_w = (narrow_all[member, 0], narrow_all[member, 1])
        peer_last_v, peer_last_w = (narrow_all[member, 2], narrow_all[member, 3])
        shrink = 1.0 - peer_first_v * beta_now
        alpha_new = (
            peer_last_u
            - peer_last_u * peer_first_v * beta_now
            + peer_last_v * alpha_now
            + peer_last_v * peer_first_u * beta_now
        ) / shrink
        beta_new = (
            peer_last_w
            - peer_last_w * peer_first_v * beta_now
            + peer_last_v * peer_first_w * beta_now
        ) / shrink
        alpha_now, beta_now = (alpha_new, beta_new)
    next_first = wide_zero
    firsts = [None] * chain_count
    nexts = [None] * chain_count
    for member in range(chain_count - 1, -1, -1):
        nexts[member] = next_first
        peer_first_u = wide_all[member, 0]
        peer_first_v, peer_first_w = (narrow_all[member, 0], narrow_all[member, 1])
        next_first = (peer_first_u + peer_first_v * alphas[member] + peer_first_w * next_first) / (
            1.0 - peer_first_v * betas[member]
        )
        firsts[member] = next_first
    alpha_prev = lax.dynamic_index_in_dim(jnp.stack(alphas), radial_at, 0, keepdims=False)
    beta_prev = lax.dynamic_index_in_dim(jnp.stack(betas), radial_at, 0, keepdims=False)
    own_first = lax.dynamic_index_in_dim(jnp.stack(firsts), radial_at, 0, keepdims=False)
    next_first = lax.dynamic_index_in_dim(jnp.stack(nexts), radial_at, 0, keepdims=False)
    prev_last = alpha_prev + beta_prev * own_first
    outputs = []
    for shell_at in range(shell_count):
        outputs.append(
            solved_u[shell_at] + prev_last * solved_v[shell_at] + next_first * solved_w[shell_at]
        )
    return jnp.stack(outputs, axis=2)


def solution(mesh):
    placed = (P("mode", None, "radial", None, None), P("mode", None, "radial"), P(), P(), P())
    return jax.shard_map(
        body,
        mesh=mesh,
        in_specs=placed,
        out_specs=P("mode", None, "radial", None, None),
        check_vma=False,
    )
```

profile of v0, /device:TPU:0, one launch (start us, length us, event | category | flops | bytes accessed | tf_op | source)
XLA Modules:
  0.0 39.1 jit_solution(3791041279454272241)
XLA Ops:
  0.0 0.7 %copy-done.4 = s32[64]{0:T(128)S(1)} copy-done((s32[64]{0:T(128)S(1)}, s32[64]{0:T(128)}, u32[]{:S(2)}) %copy-start.4) | copy-done | bytes 280
  1.4 0.4 copy.85
  1.8 1.0 %reshape.1034 = bf16[32,2,192]{2,1,0:T(2,128)(2,1)} reshape(bf16[256,3,2,8]{3,2,1,0:T(2,128)(2,1)S(1)} %bitcast.154) | data formatting | bytes 49152
  2.8 7.3 %all-to-all-start = ((bf16[32,2,192]{2,1,0:T(2,128)(2,1)}), bf16[32,2,192]{2,1,0:T(2,128)(2,1)S(1)}, u32[]{:S(2)}, u32[]{:S(2)}) async-start(bf16[32,2,192]{2,1,0:T(2,128)(2,1)} %reshape.1034), calls=%async_computation | async-start | bytes 65536 | tf_op jit(solution)/shard_map/all_to_all | solution.py:76
  10.1 0.7 %collective-permute-start = (bf16[2,3,1,2,129]{4,1,3,0,2:T(4,128)(2,1)S(1)}, bf16[2,3,1,2,129]{4,1,3,0,2:T(4,128)(2,1)S(1)}, u32[]{:S(2)}, u32[]{:S(2)}) collective-permute-start(bf16[2,3,1,2,129]{4,1,3,0,2:T(4,128)(2,1)S(1)} %get-tuple-element.20), channel_id=1, source_target_pairs={} | collective-permute-start | bytes 9296 | tf_op jit(solution)/shard_map/ppermute | solution.py:19
  10.8 0.7 %collective-permute-start.1 = (bf16[2,3,1,2,129]{4,1,3,0,2:T(4,128)(2,1)S(1)}, bf16[2,3,1,2,129]{4,1,3,0,2:T(4,128)(2,1)S(1)}, u32[]{:S(2)}, u32[]{:S(2)}) collective-permute-start(bf16[2,3,1,2,129]{4,1,3,0,2:T(4,128)(2,1)S(1)} %get-tuple-element.21), channel_id=1, source_target_pairs={} | collective-permute-start | bytes 9296 | tf_op jit(solution)/shard_map/ppermute | solution.py:20
  11.7 0.6 %copy-done.2 = f32[3]{0:T(128)S(1)} copy-done((f32[3]{0:T(128)S(1)}, f32[3]{0:T(128)}, u32[]{:S(2)}) %copy-start.2) | copy-done | bytes 36
  13.0 4.3 %all-to-all-done = bf16[32,2,192]{2,1,0:T(2,128)(2,1)S(1)} async-done(((bf16[32,2,192]{2,1,0:T(2,128)(2,1)}), bf16[32,2,192]{2,1,0:T(2,128)(2,1)S(1)}, u32[]{:S(2)}, u32[]{:S(2)}) %all-to-all-start) | async-done | bytes 24608 | tf_op jit(solution)/shard_map/all_to_all | solution.py:76
  17.3 0.3 reshape.1035
  17.9 0.5 %reshape.1029 = f32[32,8,2,3,8]{1,0,4,3,2:T(8,128)S(1)} reshape(bf16[256,2,3,8]{0,3,2,1:T(8,128)(2,1)S(1)} %copy.86) | data formatting | bytes 73728 | tf_op jit(solution)/shard_map/convert_element_type | solution.py:86
  18.4 0.9 %copy.87 = f32[8,2,3,32,8]{4,3,0,2,1:T(8,128)S(1)} copy(f32[8,2,3,32,8]{0,3,4,2,1:T(8,128)S(1)} %bitcast.152) | data formatting | bytes 98304 | tf_op jit(solution)/shard_map/convert_element_type | solution.py:86
  19.3 0.4 %reshape.1028 = f32[8,2,3,256]{3,0,2,1:T(8,128)S(1)} reshape(f32[8,2,3,32,8]{4,3,0,2,1:T(8,128)S(1)} %copy.87) | data formatting | bytes 98304 | tf_op jit(solution)/shard_map/convert_element_type | solution.py:86
  19.7 2.0 %fusion.6 = f32[8,2,3,384]{3,0,2,1:T(8,128)S(1)} fusion(s32[256]{0:T(256)S(1)} %reshape.1025, pred[256]{0:T(512)(128)(4,1)S(1)} %broadcast_in_dim.121, f32[8,2,3,256]{3,0,2,1:T(8,128)S(1)} %reshape.1028, f32[256]{0:T(256)S(1)} %compare_select_fusion.5), kind=kOutput, calls=%fused_computation.10 | convolution fusion | flops 57716736 | bytes 125184 | tf_op jit(solution)/shard_map/dot_general | solution.py:93
  21.8 2.1 %fusion.3 = bf16[48,256]{1,0:T(8,128)(2,1)S(1)} fusion(f32[48,384]{1,0:T(8,128)S(1)} %reshape.1026, s32[256]{0:T(256)S(1)} %reshape.1025, pred[256]{0:T(512)(128)(4,1)S(1)} %broadcast_in_dim.121), kind=kOutput, calls=%fused_computation.6 | convolution fusion | flops 57729024 | bytes 99584 | tf_op jit(solution)/shard_map/dot_general | solution.py:103
  24.0 0.4 copy.89
  24.4 1.0 %reshape.1036 = bf16[32,2,192]{2,1,0:T(2,128)(2,1)} reshape(bf16[256,3,2,8]{3,2,1,0:T(2,128)(2,1)S(1)} %bitcast.157) | data formatting | bytes 49152
  25.4 2.5 %all-to-all-start.1 = ((bf16[32,2,192]{2,1,0:T(2,128)(2,1)}), bf16[32,2,192]{2,1,0:T(2,128)(2,1)S(1)}, u32[]{:S(2)}, u32[]{:S(2)}) async-start(bf16[32,2,192]{2,1,0:T(2,128)(2,1)} %reshape.1036), calls=%async_computation.1 | async-start | bytes 65536 | tf_op jit(solution)/shard_map/all_to_all | solution.py:110
  28.0 7.2 %all-to-all-done.1 = bf16[32,2,192]{2,1,0:T(2,128)(2,1)S(1)} async-done(((bf16[32,2,192]{2,1,0:T(2,128)(2,1)}), bf16[32,2,192]{2,1,0:T(2,128)(2,1)S(1)}, u32[]{:S(2)}, u32[]{:S(2)}) %all-to-all-start.1) | async-done | bytes 24608 | tf_op jit(solution)/shard_map/all_to_all | solution.py:110
  35.2 0.3 reshape.1037
  35.5 0.6 %copy.108 = bf16[8,2,3,32,8]{4,3,0,2,1:T(8,128)(2,1)S(1)} copy(bf16[8,2,3,32,8]{0,1,2,4,3:T(2,128)(2,1)S(1)} %bitcast.156) | data formatting | bytes 49152 | tf_op jit(solution)/shard_map/all_to_all | solution.py:110
  36.1 0.3 copy.91
  36.6 0.3 copy.94
  37.6 0.6 %copy-done.3 = f32[3]{0:T(128)S(1)} copy-done((f32[3]{0:T(128)S(1)}, f32[3]{0:T(128)}, u32[]{:S(2)}) %copy-start.3) | copy-done | bytes 36
  38.5 0.6 %copy.99 = f32[2,3,2,2,129]{4,3,2,1,0:T(2,128)} copy(f32[2,3,2,2,129]{4,1,3,0,2:T(4,128)S(1)} %pad_maximum_fusion.1) | data formatting | bytes 24768 | tf_op jit(solution)/shard_map/stack | solution.py:232
  (56 shorter events, 3.1 us)
Async XLA Ops:
  0.0 1.0 %copy-start = (bf16[2,129,128]{2,0,1:T(2,128)(2,1)S(1)}, bf16[2,129,128]{2,0,1:T(2,128)(2,1)}, u32[]{:S(2)}) copy-start(bf16[2,129,128]{2,0,1:T(2,128)(2,1)} %param.6) | copy-start | bytes 198148
  0.0 0.7 %copy-start.4 = (s32[64]{0:T(128)S(1)}, s32[64]{0:T(128)}, u32[]{:S(2)}) copy-start(s32[64]{0:T(128)} %param.7) | copy-start | bytes 772
  0.0 0.9 %copy-start.1 = (f32[2,3,2,2,129]{4,3,2,1,0:T(2,128)S(1)}, f32[2,3,2,2,129]{4,3,2,1,0:T(2,128)}, u32[]{:S(2)}) copy-start(f32[2,3,2,2,129]{4,3,2,1,0:T(2,128)} %param.5) | copy-start | bytes 37156
  2.8 14.6 %all-to-all-start = ((bf16[32,2,192]{2,1,0:T(2,128)(2,1)}), bf16[32,2,192]{2,1,0:T(2,128)(2,1)S(1)}, u32[]{:S(2)}, u32[]{:S(2)}) async-start(bf16[32,2,192]{2,1,0:T(2,128)(2,1)} %reshape.1034), calls=%async_computation | async-start | bytes 65536 | tf_op jit(solution)/shard_map/all_to_all | solution.py:76
  10.1 17.8 %collective-permute-start = (bf16[2,3,1,2,129]{4,1,3,0,2:T(4,128)(2,1)S(1)}, bf16[2,3,1,2,129]{4,1,3,0,2:T(4,128)(2,1)S(1)}, u32[]{:S(2)}, u32[]{:S(2)}) collective-permute-start(bf16[2,3,1,2,129]{4,1,3,0,2:T(4,128)(2,1)S(1)} %get-tuple-element.20), channel_id=1, source_target_pairs={} | collective-permute-start | bytes 9296 | tf_op jit(solution)/shard_map/ppermute | solution.py:19
  10.8 17.2 %collective-permute-start.1 = (bf16[2,3,1,2,129]{4,1,3,0,2:T(4,128)(2,1)S(1)}, bf16[2,3,1,2,129]{4,1,3,0,2:T(4,128)(2,1)S(1)}, u32[]{:S(2)}, u32[]{:S(2)}) collective-permute-start(bf16[2,3,1,2,129]{4,1,3,0,2:T(4,128)(2,1)S(1)} %get-tuple-element.21), channel_id=1, source_target_pairs={} | collective-permute-start | bytes 9296 | tf_op jit(solution)/shard_map/ppermute | solution.py:20
  11.6 0.7 %copy-start.2 = (f32[3]{0:T(128)S(1)}, f32[3]{0:T(128)}, u32[]{:S(2)}) copy-start(f32[3]{0:T(128)} %param.8) | copy-start | bytes 40
  25.4 9.8 %all-to-all-start.1 = ((bf16[32,2,192]{2,1,0:T(2,128)(2,1)}), bf16[32,2,192]{2,1,0:T(2,128)(2,1)S(1)}, u32[]{:S(2)}, u32[]{:S(2)}) async-start(bf16[32,2,192]{2,1,0:T(2,128)(2,1)} %reshape.1036), calls=%async_computation.1 | async-start | bytes 65536 | tf_op jit(solution)/shard_map/all_to_all | solution.py:110
  37.6 0.7 %copy-start.3 = (f32[3]{0:T(128)S(1)}, f32[3]{0:T(128)}, u32[]{:S(2)}) copy-start(f32[3]{0:T(128)} %param.9) | copy-start | bytes 40
where the time goes:
time: 39.4 us; the launch traced here: 39.1 us
  waiting for transfers between devices  11.5 us (29%)
  starting transfers between devices  11.2 us (28%)
  local copies, waits for them, and re-layouts  10.3 us (26%)
  matrix products  4.71 us (12%)
  other arithmetic  1.02 us (3%)
  between operations  0.42 us (1%)
    all_to_all x1, starting transfers between devices, body(): lax.all_to_all(joined.reshape(lat_total, shell_count, coeffs.shape[1], 4...  7.33 us
    all_to_all x1, waiting for transfers between devices, body(): lax.all_to_all(answers.reshape(lat_dev, item_count, field_count, column_c...  7.2 us
    unnamed x15, local copies, waits for them, and re-layouts  4.52 us
    all_to_all x1, waiting for transfers between devices, body(): lax.all_to_all(joined.reshape(lat_total, shell_count, coeffs.shape[1], 4...  4.32 us
    all_to_all x1, starting transfers between devices, body(): lax.all_to_all(answers.reshape(lat_dev, item_count, field_count, column_c...  2.52 us
    dot_general x1, matrix products, body(): lax.dot_general(products.reshape(row_total, block_size), wave_table, (((1...  2.15 us
    dot_general x1, matrix products, body(): values = jnp.dot(weighted, wave_table, precision=lax.Precision.HIGHEST)  2.03 us
    convert_element_type x3, local copies, waits for them, and re-layouts, body(): pieces.reshape(row_total, column_count).astype(jnp.float32)  1.73 us
  transfers between devices with their start and end apart: 4, of which 2 were waited for; matrix products, arithmetic and copies ran while one was open for 23% of the time, Pallas kernels for 0%

commit v1 on v0

--- a/solution.py
+++ b/solution.py
@@ -1,12 +1,24 @@
+import functools
 import math
 import jax
 import jax.numpy as jnp
 from jax import lax
 from jax.sharding import PartitionSpec as P
+from jax.lax import all_to_all, axis_size
 
 inner_radius = 0.538
 shell_step = 1.0 / 2048.0
 block_limit = 384
+
+
+def note_ranges(chunk, dimension_no, k_dim):
+    return jnp.concatenate(
+        all_to_all(jnp.stack(jnp.split(chunk, axis_size("mode"), dimension_no), 0), "mode", 0, 0),
+        k_dim,
+    )
+
+
+regions_save = functools.partial(note_ranges, dimension_no=3, k_dim=0)
 
 
 def with_halo(shard, sides, width):
@@ -107,13 +119,7 @@
             precision=lax.Precision.HIGHEST,
         )
     answers = (totals * analysis_scale).astype(jnp.bfloat16)
-    returned = lax.all_to_all(
-        answers.reshape(lat_dev, item_count, field_count, column_count),
-        "mode",
-        split_axis=3,
-        concat_axis=0,
-        tiled=True,
-    )
+    returned = regions_save(answers.reshape(lat_dev, item_count, field_count, column_count))
     subset_fields = returned.shape[2]
     arranged = returned.reshape(lat_total, shell_count, subset_fields, part_count, pairs_dev, 2)
     from_north = jnp.einsum(

time: 39.4 us -> 41.2 us (1.046)
  local copies, waits for them, and re-layouts: 10.3 us -> 12 us
    unnamed x15 -> x46, local copies, waits for them, and re-layouts: 4.52 us -> 7.14 us
    all_to_all x1 -> x0, local copies, waits for them, and re-layouts: 0.55 us -> none  [body(): lax.all_to_all(answers.reshape(lat_dev, item_count, field_count, column_c...]
  transfers between devices with their start and end apart: 4 -> 4, of which waited for: 2 -> 2; matrix products, arithmetic and copies ran while one was open for 23% -> 28% of each run, Pallas kernels for 0% -> 0%
where the time goes in v1:
time: 41.2 us; the launch traced here: 41 us
  local copies, waits for them, and re-layouts  12 us (29%)
  waiting for transfers between devices  11.5 us (28%)
  starting transfers between devices  11.2 us (27%)
  matrix products  4.71 us (11%)
  other arithmetic  1.02 us (2%)
  between operations  0.54 us (1%)
    all_to_all x1, starting transfers between devices, body(): lax.all_to_all(joined.reshape(lat_total, shell_count, coeffs.shape[1], 4...  7.33 us
    all_to_all x1, waiting for transfers between devices, note_ranges(): all_to_all(jnp.stack(jnp.split(chunk, axis_size('mode'), dimension_no), 0...  7.2 us
    unnamed x46, local copies, waits for them, and re-layouts  7.14 us
    all_to_all x1, waiting for transfers between devices, body(): lax.all_to_all(joined.reshape(lat_total, shell_count, coeffs.shape[1], 4...  4.32 us
    all_to_all x1, starting transfers between devices, note_ranges(): all_to_all(jnp.stack(jnp.split(chunk, axis_size('mode'), dimension_no), 0...  2.52 us
    dot_general x1, matrix products, body(): lax.dot_general(products.reshape(row_total, block_size), wave_table, (((1...  2.15 us
    dot_general x1, matrix products, body(): values = jnp.dot(weighted, wave_table, precision=lax.Precision.HIGHEST)  2.03 us
    convert_element_type x3, local copies, waits for them, and re-layouts, body(): pieces.reshape(row_total, column_count).astype(jnp.float32)  1.73 us
  transfers between devices with their start and end apart: 4, of which 2 were waited for; matrix products, arithmetic and copies ran while one was open for 28% of the time, Pallas kernels for 0%

profile of v1, /device:TPU:0, one launch (start us, length us, event | category | flops | bytes accessed | tf_op | source)
XLA Modules:
  0.0 41.0 jit_solution(5366070116452455514)
XLA Ops:
  0.0 0.7 %copy-done.4 = s32[64]{0:T(128)S(1)} copy-done((s32[64]{0:T(128)S(1)}, s32[64]{0:T(128)}, u32[]{:S(2)}) %copy-start.4) | copy-done | bytes 280
  1.4 0.4 copy.165
  1.8 1.0 %reshape.1032 = bf16[32,2,192]{2,1,0:T(2,128)(2,1)} reshape(bf16[256,3,2,8]{3,2,1,0:T(2,128)(2,1)S(1)} %bitcast.282) | data formatting | bytes 49152
  2.8 7.3 %all-to-all-start = ((bf16[32,2,192]{2,1,0:T(2,128)(2,1)}), bf16[32,2,192]{2,1,0:T(2,128)(2,1)S(1)}, u32[]{:S(2)}, u32[]{:S(2)}) async-start(bf16[32,2,192]{2,1,0:T(2,128)(2,1)} %reshape.1032), calls=%async_computation | async-start | bytes 65536 | tf_op jit(solution)/shard_map/all_to_all | solution.py:88
  10.1 0.7 %collective-permute-start = (bf16[2,3,1,2,129]{4,1,3,0,2:T(4,128)(2,1)S(1)}, bf16[2,3,1,2,129]{4,1,3,0,2:T(4,128)(2,1)S(1)}, u32[]{:S(2)}, u32[]{:S(2)}) collective-permute-start(bf16[2,3,1,2,129]{4,1,3,0,2:T(4,128)(2,1)S(1)} %get-tuple-element.20), channel_id=1, source_target_pairs={} | collective-permute-start | bytes 9296 | tf_op jit(solution)/shard_map/ppermute | solution.py:31
  10.8 0.7 %collective-permute-start.1 = (bf16[2,3,1,2,129]{4,1,3,0,2:T(4,128)(2,1)S(1)}, bf16[2,3,1,2,129]{4,1,3,0,2:T(4,128)(2,1)S(1)}, u32[]{:S(2)}, u32[]{:S(2)}) collective-permute-start(bf16[2,3,1,2,129]{4,1,3,0,2:T(4,128)(2,1)S(1)} %get-tuple-element.21), channel_id=1, source_target_pairs={} | collective-permute-start | bytes 9296 | tf_op jit(solution)/shard_map/ppermute | solution.py:32
  11.7 0.6 %copy-done.2 = f32[3]{0:T(128)S(1)} copy-done((f32[3]{0:T(128)S(1)}, f32[3]{0:T(128)}, u32[]{:S(2)}) %copy-start.2) | copy-done | bytes 36
  13.0 4.3 %all-to-all-done = bf16[32,2,192]{2,1,0:T(2,128)(2,1)S(1)} async-done(((bf16[32,2,192]{2,1,0:T(2,128)(2,1)}), bf16[32,2,192]{2,1,0:T(2,128)(2,1)S(1)}, u32[]{:S(2)}, u32[]{:S(2)}) %all-to-all-start) | async-done | bytes 24608 | tf_op jit(solution)/shard_map/all_to_all | solution.py:88
  17.3 0.3 reshape.1033
  17.7 0.3 copy.166
  17.9 0.5 %reshape.1027 = f32[32,8,2,3,8]{1,0,4,3,2:T(8,128)S(1)} reshape(bf16[256,2,3,8]{0,3,2,1:T(8,128)(2,1)S(1)} %copy.166) | data formatting | bytes 73728 | tf_op jit(solution)/shard_map/convert_element_type | solution.py:98
  18.4 0.9 %copy.167 = f32[8,2,3,32,8]{4,3,0,2,1:T(8,128)S(1)} copy(f32[8,2,3,32,8]{0,3,4,2,1:T(8,128)S(1)} %bitcast.280) | data formatting | bytes 98304 | tf_op jit(solution)/shard_map/convert_element_type | solution.py:98
  19.3 0.4 reshape.1026
  19.7 2.0 %fusion.6 = f32[8,2,3,384]{3,0,2,1:T(8,128)S(1)} fusion(s32[256]{0:T(256)S(1)} %reshape.1023, pred[256]{0:T(512)(128)(4,1)S(1)} %broadcast_in_dim.121, f32[8,2,3,256]{3,0,2,1:T(8,128)S(1)} %reshape.1026, f32[256]{0:T(256)S(1)} %compare_select_fusion.5), kind=kOutput, calls=%fused_computation.10 | convolution fusion | flops 57716736 | bytes 125184 | tf_op jit(solution)/shard_map/dot_general | solution.py:105
  21.8 2.1 %fusion.3 = bf16[48,256]{1,0:T(8,128)(2,1)S(1)} fusion(f32[48,384]{1,0:T(8,128)S(1)} %reshape.1024, s32[256]{0:T(256)S(1)} %reshape.1023, pred[256]{0:T(512)(128)(4,1)S(1)} %broadcast_in_dim.121), kind=kOutput, calls=%fused_computation.6 | convolution fusion | flops 57729024 | bytes 99584 | tf_op jit(solution)/shard_map/dot_general | solution.py:115
  26.9 1.0 %reshape.1034 = bf16[32,2,192]{2,1,0:T(2,128)(2,1)} reshape(bf16[32,2,3,8,8]{4,3,2,1,0:T(8,128)(2,1)S(1)} %bitcast.284) | data formatting | bytes 49152
  27.9 2.5 %all-to-all-start.1 = ((bf16[32,2,192]{2,1,0:T(2,128)(2,1)}), bf16[32,2,192]{2,1,0:T(2,128)(2,1)S(1)}, u32[]{:S(2)}, u32[]{:S(2)}) async-start(bf16[32,2,192]{2,1,0:T(2,128)(2,1)} %reshape.1034), calls=%async_computation.1 | async-start | bytes 65536 | tf_op jit(solution)/shard_map/all_to_all | solution.py:16
  30.5 7.2 %all-to-all-done.1 = bf16[32,2,192]{2,1,0:T(2,128)(2,1)S(1)} async-done(((bf16[32,2,192]{2,1,0:T(2,128)(2,1)}), bf16[32,2,192]{2,1,0:T(2,128)(2,1)S(1)}, u32[]{:S(2)}, u32[]{:S(2)}) %all-to-all-start.1) | async-done | bytes 24608 | tf_op jit(solution)/shard_map/all_to_all | solution.py:16
  37.7 0.3 reshape.1035
  38.1 0.2 copy.170
  38.3 0.2 slice.78
  38.5 0.2 copy.173
  39.4 0.6 %copy-done.3 = f32[3]{0:T(128)S(1)} copy-done((f32[3]{0:T(128)S(1)}, f32[3]{0:T(128)}, u32[]{:S(2)}) %copy-start.3) | copy-done | bytes 36
  40.3 0.6 %copy.178 = f32[2,3,2,2,129]{4,3,2,1,0:T(2,128)} copy(f32[2,3,2,2,129]{4,1,3,0,2:T(4,128)S(1)} %pad_maximum_fusion.1) | data formatting | bytes 24768 | tf_op jit(solution)/shard_map/stack | solution.py:238
  (87 shorter events, 5.4 us)
Async XLA Ops:
  0.0 1.0 %copy-start = (bf16[2,129,128]{2,0,1:T(2,128)(2,1)S(1)}, bf16[2,129,128]{2,0,1:T(2,128)(2,1)}, u32[]{:S(2)}) copy-start(bf16[2,129,128]{2,0,1:T(2,128)(2,1)} %param.6) | copy-start | bytes 198148
  0.0 0.7 %copy-start.4 = (s32[64]{0:T(128)S(1)}, s32[64]{0:T(128)}, u32[]{:S(2)}) copy-start(s32[64]{0:T(128)} %param.7) | copy-start | bytes 772
  0.0 0.9 %copy-start.1 = (f32[2,3,2,2,129]{4,3,2,1,0:T(2,128)S(1)}, f32[2,3,2,2,129]{4,3,2,1,0:T(2,128)}, u32[]{:S(2)}) copy-start(f32[2,3,2,2,129]{4,3,2,1,0:T(2,128)} %param.5) | copy-start | bytes 37156
  2.8 14.6 %all-to-all-start = ((bf16[32,2,192]{2,1,0:T(2,128)(2,1)}), bf16[32,2,192]{2,1,0:T(2,128)(2,1)S(1)}, u32[]{:S(2)}, u32[]{:S(2)}) async-start(bf16[32,2,192]{2,1,0:T(2,128)(2,1)} %reshape.1032), calls=%async_computation | async-start | bytes 65536 | tf_op jit(solution)/shard_map/all_to_all | solution.py:88
  10.1 20.3 %collective-permute-start = (bf16[2,3,1,2,129]{4,1,3,0,2:T(4,128)(2,1)S(1)}, bf16[2,3,1,2,129]{4,1,3,0,2:T(4,128)(2,1)S(1)}, u32[]{:S(2)}, u32[]{:S(2)}) collective-permute-start(bf16[2,3,1,2,129]{4,1,3,0,2:T(4,128)(2,1)S(1)} %get-tuple-element.20), channel_id=1, source_target_pairs={} | collective-permute-start | bytes 9296 | tf_op jit(solution)/shard_map/ppermute | solution.py:31
  10.8 19.7 %collective-permute-start.1 = (bf16[2,3,1,2,129]{4,1,3,0,2:T(4,128)(2,1)S(1)}, bf16[2,3,1,2,129]{4,1,3,0,2:T(4,128)(2,1)S(1)}, u32[]{:S(2)}, u32[]{:S(2)}) collective-permute-start(bf16[2,3,1,2,129]{4,1,3,0,2:T(4,128)(2,1)S(1)} %get-tuple-element.21), channel_id=1, source_target_pairs={} | collective-permute-start | bytes 9296 | tf_op jit(solution)/shard_map/ppermute | solution.py:32
  11.6 0.7 %copy-start.2 = (f32[3]{0:T(128)S(1)}, f32[3]{0:T(128)}, u32[]{:S(2)}) copy-start(f32[3]{0:T(128)} %param.8) | copy-start | bytes 40
  27.9 9.8 %all-to-all-start.1 = ((bf16[32,2,192]{2,1,0:T(2,128)(2,1)}), bf16[32,2,192]{2,1,0:T(2,128)(2,1)S(1)}, u32[]{:S(2)}, u32[]{:S(2)}) async-start(bf16[32,2,192]{2,1,0:T(2,128)(2,1)} %reshape.1034), calls=%async_computation.1 | async-start | bytes 65536 | tf_op jit(solution)/shard_map/all_to_all | solution.py:16
  39.4 0.7 %copy-start.3 = (f32[3]{0:T(128)S(1)}, f32[3]{0:T(128)}, u32[]{:S(2)}) copy-start(f32[3]{0:T(128)} %param.9) | copy-start | bytes 40
